TPU v7x, 128 devices: a whole 4x4x4 slice. The times are simulated.
128 devices in a mesh: req: 8 (over y, core), exp: 16 (over x, z).
Axes of the slice: x: 4, y: 4, z: 4, core: 2. Of those that a mesh axis runs over, the one named last changes fastest.
Arguments:
- tokens: bfloat16 [49152, 1536], P(('req', 'exp')), may hold values from -30 to 30
- segment_lengths: int32 [8, 16], P('req'), may hold values from 1 to 3071, as said below
- segment_adapters: int32 [8, 16], P('req'), may hold values from 0 to 15
- routes: int32 [49152, 4], P(('req', 'exp')), may hold values from 0 to 31, all different within a row; in each aligned block of 384 rows (0 to 383, 384 to 767, ...) at most 64 rows name the same one
- gate_weights: float32 [49152, 4], P(('req', 'exp')), may hold values from 0.05 to 1
- attention_gain: float32 [1536], replicated, may hold values from 0.5 to 1.5
- attention_in: bfloat16 [1536, 2048], P(None, 'req'), may hold values from -5 to 5
- sink_logits: float32 [12], replicated, may hold values from 0 to 6
- attention_out: bfloat16 [1536, 1536], P(None, 'req'), may hold values from -0.15625 to 0.15625
- expert_gain: float32 [1536], replicated, may hold values from 0.5 to 1.5
- expert_gate_up: bfloat16 [32, 1536, 1536], P('exp'), may hold values from -0.15625 to 0.15625
- expert_down: bfloat16 [32, 768, 1536], P('exp'), may hold values from -0.21875 to 0.21875
- adapter_in_down: bfloat16 [16, 1536, 16], P('req'), may hold values from -0.15625 to 0.15625
- adapter_in_up: bfloat16 [16, 16, 2048], P('req'), may hold values from -0.625 to 0.625
- adapter_out_down: bfloat16 [16, 1536, 16], P('req'), may hold values from -0.15625 to 0.15625
- adapter_out_up: bfloat16 [16, 16, 1536], P('req'), may hold values from -0.625 to 0.625
- adapter_expert_down: bfloat16 [16, 1536, 16], P('req'), may hold values from -0.15625 to 0.15625
- adapter_expert_up: bfloat16 [16, 32, 16, 768], P('req', 'exp'), may hold values from -0.625 to 0.625
Outputs:
- layer_output: bfloat16 [49152, 1536], P(('req', 'exp'))
Inputs may be any that keep to these rules, and one draw needn't show every extreme that they name: `segment_lengths`: each row sums to 6144; entry 0 is the group's shared prompt of 1536 to 3071 tokens, the other entries are its requests, none longer than the prompt's most. `routes`: in each aligned block of 384 token rows (the rows of one device) no expert is named more than 64 times, a bound that some block reaches; a row names 4 different experts.
All inputs are finite; a program needn't handle non-finite values.
Results may differ from a plain program's by a relative error of at most 0.012.
The roundings to bfloat16 on the way count: a program that leaves them out, or rounds other values in their place, can miss the bound.
Values may be sent and summed in bfloat16 or wider, within the bound.
A program may use at most 128 MiB of HBM per device.

v0:
```python
import jax
import jax.numpy as jnp
from jax import lax
from jax.sharding import PartitionSpec as P

HEADS = 12
KVH = 2
HD = 128
EXPERTS = 32
WINDOW = 4096
CAP = 64
EPSILON = 1e-06
NEGATIVE = -1e30


def scaled_norm(inputs, gain):
    floats = inputs.astype(jnp.float32)
    inverse = lax.rsqrt(jnp.mean(floats * floats, axis=-1, keepdims=True) + EPSILON)
    return (floats * inverse * gain).astype(jnp.bfloat16)


def segment_of(positions, lengths):
    seg_ends = jnp.cumsum(lengths)
    return jnp.sum((positions[:, None] >= seg_ends[None, :]).astype(jnp.int32), axis=1)


def adapter_select(token_adapter, adapter_count, rank_size):
    owners = jnp.repeat(jnp.arange(adapter_count, dtype=jnp.int32), rank_size)
    return token_adapter[:, None] == owners[None, :]


def low_coords(inputs, select, first_factor):
    adapter_count, inner_width, rank_size = first_factor.shape
    joined = jnp.transpose(first_factor, (1, 0, 2)).reshape(inner_width, adapter_count * rank_size)
    coords = jnp.dot(inputs, joined, preferred_element_type=jnp.float32)
    return jnp.where(select, coords, 0.0).astype(jnp.bfloat16)


def low_rank(inputs, select, first_factor, second_factor):
    coords = low_coords(inputs, select, first_factor)
    adapter_count, rank_size, outer_width = second_factor.shape
    return jnp.dot(
        coords,
        second_factor.reshape(adapter_count * rank_size, outer_width),
        preferred_element_type=jnp.float32,
    )


def online_step(softmax_state, queries, key_piece, positions, segments, key_pos, lengths):
    running_max, running_sum, weighted = softmax_state
    key_heads = queries.shape[1]
    head_size = queries.shape[3]
    key_part = key_piece[:, : key_heads * head_size].reshape(-1, key_heads, head_size)
    value_part = key_piece[:, key_heads * head_size :].reshape(-1, key_heads, head_size)
    scores = jnp.einsum(
        "tkgd,skd->tkgs", queries, key_part, preferred_element_type=jnp.float32
    ) * head_size ** (-0.5)
    key_seg = segment_of(key_pos, lengths)
    allowed = (
        (key_pos[None, :] <= positions[:, None])
        & (positions[:, None] - key_pos[None, :] < WINDOW)
        & (key_pos[None, :] >= 0)
    )
    allowed = allowed & ((key_seg[None, :] == segments[:, None]) | (key_seg[None, :] == 0))
    scores = jnp.where(allowed[:, None, None, :], scores, NEGATIVE)
    new_max = jnp.maximum(running_max, jnp.max(scores, axis=-1))
    factor = jnp.exp(running_max - new_max)
    weights = jnp.exp(scores - new_max[..., None])
    running_sum = running_sum * factor + jnp.sum(weights, axis=-1)
    weighted = weighted * factor[..., None] + jnp.einsum(
        "tkgs,skd->tkgd",
        weights.astype(jnp.bfloat16),
        value_part,
        preferred_element_type=jnp.float32,
    )
    return (new_max, running_sum, weighted)


def body(
    tokens,
    segment_lengths,
    segment_adapters,
    routes,
    gate_weights,
    attention_gain,
    attention_in,
    sink_logits,
    attention_out,
    expert_gain,
    expert_gate_up,
    expert_down,
    adapter_in_down,
    adapter_in_up,
    adapter_out_down,
    adapter_out_up,
    adapter_expert_down,
    adapter_expert_up,
):
    tok_rows = tokens.shape[0]
    lengths = segment_lengths[0]
    segment_total = lengths.shape[0]
    first_pos = lax.axis_index("exp") * tok_rows
    positions = first_pos + jnp.arange(tok_rows, dtype=jnp.int32)
    segments = segment_of(positions, lengths)
    matches = segments[:, None] == jnp.arange(segment_total, dtype=jnp.int32)[None, :]
    token_adapter = jnp.sum(jnp.where(matches, segment_adapters[0][None, :], 0), axis=1)
    held_factors = (
        lax.all_gather(adapter_in_down, "req", axis=0, tiled=True),
        lax.all_gather(adapter_in_up, "req", axis=0, tiled=True),
        lax.all_gather(adapter_out_down, "req", axis=0, tiled=True),
        lax.all_gather(adapter_out_up, "req", axis=0, tiled=True),
        lax.all_gather(adapter_expert_down, "req", axis=0, tiled=True),
        lax.all_gather(adapter_expert_up, "req", axis=0, tiled=True),
    )
    in_low, in_high, out_low, out_high, expert_low, expert_high = held_factors
    select = adapter_select(token_adapter, in_low.shape[0], in_low.shape[2])
    normed = scaled_norm(tokens, attention_gain)
    full_in, full_out = (
        lax.all_gather(attention_in, "req", axis=1, tiled=True),
        lax.all_gather(attention_out, "req", axis=1, tiled=True),
    )
    base_heads = jnp.dot(normed, full_in, preferred_element_type=jnp.float32)
    projected = (base_heads + low_rank(normed, select, in_low, in_high)).astype(jnp.bfloat16)
    group_size = HEADS // KVH
    queries = projected[:, : HEADS * HD].reshape(tok_rows, KVH, group_size, HD)
    key_value = projected[:, HEADS * HD :]
    sink_grid = jnp.broadcast_to(
        sink_logits.reshape(KVH, group_size)[None], (tok_rows, KVH, group_size)
    )
    initial = (
        sink_grid,
        jnp.ones_like(sink_grid),
        jnp.zeros((tok_rows, KVH, group_size, HD), jnp.float32),
    )
    key_piece = lax.all_gather(key_value, "exp", axis=0, tiled=True)
    piece_rows = key_piece.shape[0]
    block_rows = tok_rows
    block_count = piece_rows // block_rows
    block_rows = 2 * block_rows
    block_count = block_count // 2
    stacked = key_piece.reshape(block_count, block_rows, key_piece.shape[1])

    def visit_block(softmax_state, block_input):
        key_block, block_index = block_input
        block_start = block_index * block_rows
        key_pos = block_start + jnp.arange(block_rows, dtype=jnp.int32)

        def update(state_now):
            return online_step(state_now, queries, key_block, positions, segments, key_pos, lengths)

        def unchanged(state_now):
            return state_now

        needed = jnp.logical_and(
            block_start <= positions[-1], block_start + block_rows - 1 > positions[0] - WINDOW
        )
        return (lax.cond(needed, update, unchanged, softmax_state), None)

    softmax_state = lax.scan(
        visit_block, initial, (stacked, jnp.arange(block_count, dtype=jnp.int32))
    )[0]
    running_max, running_sum, weighted = softmax_state
    attended = (
        (weighted / running_sum[..., None]).reshape(tok_rows, HEADS * HD).astype(jnp.bfloat16)
    )
    base_out = jnp.dot(attended, full_out, preferred_element_type=jnp.float32)
    residual = (
        tokens.astype(jnp.float32) + base_out + low_rank(attended, select, out_low, out_high)
    ).astype(jnp.bfloat16)
    normed_two = scaled_norm(residual, expert_gain)
    low_parts = low_coords(normed_two, select, expert_low)
    top_count = routes.shape[1]
    picked = routes.reshape(-1)
    expert_hot = (picked[:, None] == jnp.arange(EXPERTS, dtype=jnp.int32)[None, :]).astype(
        jnp.int32
    )
    arrival = jnp.sum((jnp.cumsum(expert_hot, axis=0) - 1) * expert_hot, axis=1)
    slot_index = picked * CAP + arrival
    pick_ids = jnp.arange(picked.shape[0], dtype=jnp.int32)
    sources = jnp.full((EXPERTS * CAP,), -1, jnp.int32).at[slot_index].set(pick_ids)
    filled = (sources >= 0)[:, None]
    token_rows = jnp.maximum(sources, 0) // top_count
    peer_count = lax.axis_size("exp")
    local_experts = EXPERTS // peer_count
    send_rows = jnp.where(filled, normed_two[token_rows], 0).reshape(
        peer_count, local_experts, CAP, -1
    )
    send_low = jnp.where(filled, low_parts[token_rows], 0).reshape(
        peer_count, local_experts, CAP, -1
    )
    adapter_bank = jnp.transpose(expert_high, (1, 0, 2, 3)).reshape(
        local_experts, -1, expert_high.shape[3]
    )
    arrived_rows = lax.all_to_all(send_rows, "exp", split_axis=0, concat_axis=0, tiled=True)
    arrived_low = lax.all_to_all(send_low, "exp", split_axis=0, concat_axis=0, tiled=True)
    hidden_width = expert_down.shape[1]
    gate_up = jnp.einsum(
        "necd,edf->necf", arrived_rows, expert_gate_up, preferred_element_type=jnp.float32
    )
    up_part = gate_up[..., hidden_width:] + jnp.einsum(
        "necr,erf->necf", arrived_low, adapter_bank, preferred_element_type=jnp.float32
    )
    hidden = (jax.nn.relu(gate_up[..., :hidden_width]) * up_part).astype(jnp.bfloat16)
    outputs = jnp.einsum(
        "necf,efd->necd", hidden, expert_down, preferred_element_type=jnp.float32
    ).astype(jnp.bfloat16)
    returned = lax.all_to_all(outputs, "exp", split_axis=0, concat_axis=0, tiled=True)
    flat_back = returned.reshape(EXPERTS * CAP, -1)
    per_pick = flat_back[slot_index].astype(jnp.float32).reshape(tok_rows, top_count, -1)
    combined = jnp.sum(gate_weights[:, :, None] * per_pick, axis=1)
    return (residual.astype(jnp.float32) + combined).astype(jnp.bfloat16)


def solution(mesh):
    return jax.shard_map(
        body,
        mesh=mesh,
        in_specs=(
            P(("req", "exp"), None),
            P("req", None),
            P("req", None),
            P(("req", "exp"), None),
            P(("req", "exp"), None),
            P(),
            P(None, "req"),
            P(),
            P(None, "req"),
            P(),
            P("exp", None, None),
            P("exp", None, None),
            P("req", None, None),
            P("req", None, None),
            P("req", None, None),
            P("req", None, None),
            P("req", None, None),
            P("req", "exp", None, None),
        ),
        out_specs=P(("req", "exp"), None),
        check_vma=False,
    )
```

profile of v0, /device:TPU:100, one launch (start us, length us, event | category | flops | bytes accessed | tf_op | source)
XLA Modules:
  0.0 715.5 jit_solution(5835617143987328835)
XLA Ops:
  13.3 15.3 %all_gather.28 = bf16[16,1536,16]{1,2,0:T(8,128)(2,1)S(1)} all-gather(bf16[2,1536,16]{1,2,0:T(8,128)(2,1)} %param.34), channel_id=1, replica_groups=mesh['req'=8,'exp'=16] {'req'}, dimensions={0}, use_global_device_ids=true | all-gather | bytes 884736 | tf_op jit(solution)/shard_map/all_gather | solution.py:108
  28.6 27.7 %all-gather.5.cloned.1.call-done = bf16[1536,2048]{1,0:T(8,128)(2,1)} async-done(((bf16[1536,256]{1,0:T(8,128)(2,1)}), bf16[1536,2048]{1,0:T(8,128)(2,1)}) %all-gather.5.cloned.1.call-update) | async-done | bytes 6291472 | tf_op jit(solution)/shard_map/all_gather | solution.py:119
  63.8 18.2 %all-gather.7.cloned.1.call-done = bf16[16,16,2048]{2,1,0:T(8,128)(2,1)} async-done(((bf16[2,16,2048]{2,1,0:T(8,128)(2,1)}), bf16[16,16,2048]{2,1,0:T(8,128)(2,1)}) %all-gather.7.cloned.1.call-update) | async-done | bytes 1048592 | tf_op jit(solution)/shard_map/all_gather | solution.py:109
  89.6 9.1 %reduce-window.27 = s32[32,12,128]{2,1,0:T(8,128)S(1)} reduce-window(s32[32,12,128]{2,1,0:T(8,128)S(1)} %fusion.45, s32[]{:T(128)} %copy.156), window={size=1x1x128 pad=0_0x0_0x127_0}, to_apply=%region_12.13 | reduce-window | flops 6242304 | bytes 393220 | tf_op jit(solution)/shard_map/reduce-window.2
  107.9 14.4 %all_gather.32 = bf16[16,1536,16]{1,2,0:T(8,128)(2,1)} all-gather(bf16[2,1536,16]{1,2,0:T(8,128)(2,1)S(1)} %copy-done.7), channel_id=1, replica_groups=mesh['req'=8,'exp'=16] {'req'}, dimensions={0}, use_global_device_ids=true | all-gather | bytes 884736 | tf_op jit(solution)/shard_map/all_gather | solution.py:110
  122.3 14.9 %all_gather.33 = bf16[16,16,1536]{2,1,0:T(8,128)(2,1)} all-gather(bf16[2,16,1536]{2,1,0:T(8,128)(2,1)S(1)} %copy-done.8), channel_id=1, replica_groups=mesh['req'=8,'exp'=16] {'req'}, dimensions={0}, use_global_device_ids=true | all-gather | bytes 884736 | tf_op jit(solution)/shard_map/all_gather | solution.py:111
  157.1 203.7 %while.18 = (s32[]{:T(128)}, f32[384,2,6]{0,2,1:T(8,128)}, f32[384,2,6]{0,2,1:T(8,128)}, f32[384,2,6,128]{3,0,2,1:T(8,128)S(1)}, s32[8]{0:T(128)}, /*index=5*/s3...) while((s32[]{:T(128)}, f32[384,2,6]{0,2,1:T(8,128)}, ...), condition=%wide.region_11.12_spmd, body=%wide.region_4.11_spmd.sunk | while | flops 1854454528 | bytes 54025088 | solution.py:159
  161.1 29.1 %conditional.2 = ((f32[384,2,6]{0,2,1:T(8,128)}, f32[384,2,6]{0,2,1:T(8,128)}, f32[384,2,6,128]{3,0,2,1:T(8,128)S(1)})) conditional(s32[]{:T(128)} %convert_element_type.156, (f32[384,2,6]{0,2,1:T(8,128)}, f32[384,2,6]{0,2,1:T(8,128)}, f32[384,2,6,128]{3,0,2,1:T(8,128)S(1)}) %tuple.62, (s32[]{:T(128)}, s32[768]{0:T(1024)S(1)}, s32[384]{0:T(512)}, ...), branch_computations={%region_5.5_spmd, %region_6.10_spmd} | conditional | flops 1854454528 | bytes 54021700 | solution.py:157
  194.1 28.6 %conditional.2 = ((f32[384,2,6]{0,2,1:T(8,128)}, f32[384,2,6]{0,2,1:T(8,128)}, f32[384,2,6,128]{3,0,2,1:T(8,128)S(1)})) conditional(s32[]{:T(128)} %convert_element_type.156, (f32[384,2,6]{0,2,1:T(8,128)}, f32[384,2,6]{0,2,1:T(8,128)}, f32[384,2,6,128]{3,0,2,1:T(8,128)S(1)}) %tuple.62, (s32[]{:T(128)}, s32[768]{0:T(1024)S(1)}, s32[384]{0:T(512)}, ...), branch_computations={%region_5.5_spmd, %region_6.10_spmd} | conditional | flops 1854454528 | bytes 54021700 | solution.py:157
  226.7 28.6 %conditional.2 = ((f32[384,2,6]{0,2,1:T(8,128)}, f32[384,2,6]{0,2,1:T(8,128)}, f32[384,2,6,128]{3,0,2,1:T(8,128)S(1)})) conditional(s32[]{:T(128)} %convert_element_type.156, (f32[384,2,6]{0,2,1:T(8,128)}, f32[384,2,6]{0,2,1:T(8,128)}, f32[384,2,6,128]{3,0,2,1:T(8,128)S(1)}) %tuple.62, (s32[]{:T(128)}, s32[768]{0:T(1024)S(1)}, s32[384]{0:T(512)}, ...), branch_computations={%region_5.5_spmd, %region_6.10_spmd} | conditional | flops 1854454528 | bytes 54021700 | solution.py:157
  259.2 28.6 %conditional.2 = ((f32[384,2,6]{0,2,1:T(8,128)}, f32[384,2,6]{0,2,1:T(8,128)}, f32[384,2,6,128]{3,0,2,1:T(8,128)S(1)})) conditional(s32[]{:T(128)} %convert_element_type.156, (f32[384,2,6]{0,2,1:T(8,128)}, f32[384,2,6]{0,2,1:T(8,128)}, f32[384,2,6,128]{3,0,2,1:T(8,128)S(1)}) %tuple.62, (s32[]{:T(128)}, s32[768]{0:T(1024)S(1)}, s32[384]{0:T(512)}, ...), branch_computations={%region_5.5_spmd, %region_6.10_spmd} | conditional | flops 1854454528 | bytes 54021700 | solution.py:157
  291.7 28.6 %conditional.2 = ((f32[384,2,6]{0,2,1:T(8,128)}, f32[384,2,6]{0,2,1:T(8,128)}, f32[384,2,6,128]{3,0,2,1:T(8,128)S(1)})) conditional(s32[]{:T(128)} %convert_element_type.156, (f32[384,2,6]{0,2,1:T(8,128)}, f32[384,2,6]{0,2,1:T(8,128)}, f32[384,2,6,128]{3,0,2,1:T(8,128)S(1)}) %tuple.62, (s32[]{:T(128)}, s32[768]{0:T(1024)S(1)}, s32[384]{0:T(512)}, ...), branch_computations={%region_5.5_spmd, %region_6.10_spmd} | conditional | flops 1854454528 | bytes 54021700 | solution.py:157
  324.3 28.6 %conditional.2 = ((f32[384,2,6]{0,2,1:T(8,128)}, f32[384,2,6]{0,2,1:T(8,128)}, f32[384,2,6,128]{3,0,2,1:T(8,128)S(1)})) conditional(s32[]{:T(128)} %convert_element_type.156, (f32[384,2,6]{0,2,1:T(8,128)}, f32[384,2,6]{0,2,1:T(8,128)}, f32[384,2,6,128]{3,0,2,1:T(8,128)S(1)}) %tuple.62, (s32[]{:T(128)}, s32[768]{0:T(1024)S(1)}, s32[384]{0:T(512)}, ...), branch_computations={%region_5.5_spmd, %region_6.10_spmd} | conditional | flops 1854454528 | bytes 54021700 | solution.py:157
  374.8 10.1 %gather_fusion = bf16[2048,1536]{1,0:T(8,128)(2,1)} fusion(bf16[384,1536]{1,0:T(8,128)(2,1)S(1)} %fusion.32, s32[2048]{0:T(1024)S(1)} %copy-done.12), kind=kCustom, calls=%fused_computation | custom fusion | bytes 12591104 | tf_op jit(solution)/shard_map/gather | solution.py:185
  390.9 35.5 %all-to-all-start = ((bf16[16,2,64,1536]{3,2,1,0:T(8,128)(2,1)}), bf16[16,2,64,1536]{3,2,1,0:T(8,128)(2,1)}, u32[]{:S(2)}, u32[]{:S(2)}) async-start(bf16[16,2,64,1536]{3,2,1,0:T(8,128)(2,1)} %broadcast_select_fusion), calls=%async_computation | async-start | bytes 12582912 | tf_op jit(solution)/shard_map/all_to_all | solution.py:194
  426.4 13.7 %all_gather.34 = bf16[16,1536,16]{1,2,0:T(8,128)(2,1)S(1)} all-gather(bf16[2,1536,16]{1,2,0:T(8,128)(2,1)S(1)} %copy-done.9), channel_id=1, replica_groups=mesh['req'=8,'exp'=16] {'req'}, dimensions={0}, use_global_device_ids=true | all-gather | bytes 884736 | tf_op jit(solution)/shard_map/all_gather | solution.py:112
  440.1 13.4 %all_gather.35 = bf16[16,2,16,768]{3,2,0,1:T(8,128)(2,1)S(1)} all-gather(bf16[2,2,16,768]{3,2,0,1:T(8,128)(2,1)S(1)} %copy.118), channel_id=1, replica_groups=mesh['req'=8,'exp'=16] {'req'}, dimensions={0}, use_global_device_ids=true | all-gather | bytes 884736 | tf_op jit(solution)/shard_map/all_gather | solution.py:113
  462.7 68.9 %all-to-all-done = bf16[16,2,64,1536]{3,2,1,0:T(8,128)(2,1)} async-done(((bf16[16,2,64,1536]{3,2,1,0:T(8,128)(2,1)}), bf16[16,2,64,1536]{3,2,1,0:T(8,128)(2,1)}, u32[]{:S(2)}, u32[]{:S(2)}) %all-to-all-start) | async-done | bytes 6291488 | tf_op jit(solution)/shard_map/all_to_all | solution.py:194
  538.6 17.0 %fusion.15 = f32[16,2,64,1536]{3,2,0,1:T(8,128)} fusion(bf16[2,1536,1536]{2,1,0:T(8,128)(2,1)} %param.32, bf16[16,2,64,1536]{3,2,1,0:T(8,128)(2,1)} %all-to-all-done), kind=kOutput, calls=%fused_computation.28 | convolution fusion | flops 9663676416 | bytes 28311552 | tf_op jit(solution)/shard_map/necd,edf->necf/dot_general | solution.py:197
  555.6 11.3 %convert_bitcast_fusion = bf16[16,2,64,1536]{3,2,0,1:T(8,128)(2,1)} fusion(bf16[2,768,1536]{2,1,0:T(8,128)(2,1)} %param.33, f32[16,2,64,1536]{3,2,0,1:T(8,128)} %fusion.15, bf16[2,256,768,1]{2,1,3,0:T(8,128)(2,1)S(1)} %bitcast.121, bf16[16,2,64,256]{3,2,1,0:T(8,128)(2,1)S(1)} %all-to-all-done.1), kind=kOutput, calls=%fused_computation.34 | convolution fusion | flops 5646581760 | bytes 25427968 | tf_op jit(solution)/shard_map/necf,efd->necd/dot_general | solution.py:204
  580.9 88.9 %all-to-all-done.2 = bf16[16,2,64,1536]{3,2,1,0:T(8,128)(2,1)} async-done(((bf16[16,2,64,1536]{3,2,1,0:T(8,128)(2,1)}), bf16[16,2,64,1536]{3,2,1,0:T(8,128)(2,1)}, u32[]{:S(2)}, u32[]{:S(2)}) %all-to-all-start.2) | async-done | bytes 6291488 | tf_op jit(solution)/shard_map/all_to_all | solution.py:207
  669.8 14.0 %gather_fusion.2 = bf16[1536,1536]{1,0:T(8,128)(2,1)} fusion(bf16[2048,1536]{1,0:T(8,128)(2,1)} %bitcast.40, s32[2048]{0:T(1024)S(1)} %pad_clamp_fusion), kind=kCustom, calls=%fused_computation.2 | custom fusion | bytes 9443328 | tf_op jit(solution)/shard_map/gather | solution.py:209
  683.8 9.7 %reshape.299 = f32[384,4,1536]{2,1,0:T(4,128)} reshape(bf16[1536,1536]{1,0:T(8,128)(2,1)} %gather_fusion.2) | data formatting | bytes 14155776 | tf_op jit(solution)/shard_map/convert_element_type | solution.py:209
  693.5 12.3 %multiply_reduce_fusion = f32[384,1536]{1,0:T(8,128)} fusion(f32[384,4,1536]{2,1,0:T(4,128)} %reshape.299, f32[384,4]{1,0:T(8,128)S(1)} %copy.111), kind=kLoop, calls=%fused_computation.27 | loop fusion | flops 4128768 | bytes 11802624 | tf_op jit(solution)/shard_map/reduce_sum | solution.py:210
  (262 shorter events, 295.3 us)
Async XLA Ops:
  6.5 49.7 %all-gather.5.cloned.1.call-start = ((), (), s32[]{:S(2)}) async-start(), calls=%async_computation.3 | async-start | bytes 7077888 | tf_op jit(solution)/shard_map/all_gather | solution.py:119
  7.3 74.7 %all-gather.7.cloned.1.call-start = ((), (), s32[]{:S(2)}) async-start(), calls=%async_computation.4 | async-start | bytes 1179648 | tf_op jit(solution)/shard_map/all_gather | solution.py:109
  8.0 138.5 %all-gather.9.cloned.1.call-start = ((), (), s32[]{:S(2)}) async-start(), calls=%async_computation.5 | async-start | bytes 6684672 | tf_op jit(solution)/shard_map/all_gather | solution.py:135
  9.0 72.9 %copy-start.18 = (s32[256]{0:T(256)}, s32[256]{0:T(256)S(1)}, u32[]{:S(2)}) copy-start(s32[256]{0:T(256)S(1)} %eq.84) | copy-start | bytes 3076
  11.7 70.3 %copy-start.16 = (s32[384]{0:T(512)}, s32[384]{0:T(512)S(1)}, u32[]{:S(2)}) copy-start(s32[384]{0:T(512)S(1)} %select_reduce_fusion) | copy-start | bytes 4612
  13.3 50.5 %copy-start.21 = (f32[384]{0:T(512)}, f32[384]{0:T(512)S(1)}, u32[]{:S(2)}) copy-start(f32[384]{0:T(512)S(1)} %add_rsqrt_fusion.1) | copy-start | bytes 4612
  28.6 53.4 %copy-start = (bf16[384,1536]{1,0:T(8,128)(2,1)S(1)}, bf16[384,1536]{1,0:T(8,128)(2,1)}, u32[]{:S(2)}) copy-start(bf16[384,1536]{1,0:T(8,128)(2,1)} %param.22) | copy-start | bytes 3538948
  85.8 22.0 %copy-start.7 = (bf16[2,1536,16]{1,2,0:T(8,128)(2,1)S(1)}, bf16[2,1536,16]{1,2,0:T(8,128)(2,1)}, u32[]{:S(2)}) copy-start(bf16[2,1536,16]{1,2,0:T(8,128)(2,1)} %param.36) | copy-start | bytes 294916
  85.8 36.5 %copy-start.8 = (bf16[2,16,1536]{2,1,0:T(8,128)(2,1)S(1)}, bf16[2,16,1536]{2,1,0:T(8,128)(2,1)}, u32[]{:S(2)}) copy-start(bf16[2,16,1536]{2,1,0:T(8,128)(2,1)} %param.37) | copy-start | bytes 294916
  86.7 278.4 %all-gather.11.cloned.1.call-start = ((), (), s32[]{:S(2)}) async-start(), calls=%async_computation.6 | async-start | bytes 5308416 | tf_op jit(solution)/shard_map/all_gather | solution.py:120
  99.7 22.6 %copy-start.13 = (s32[1536]{0:T(1024)}, s32[1536]{0:T(1024)S(1)}, u32[]{:S(2)}) copy-start(s32[1536]{0:T(1024)S(1)} %fusion.56) | copy-start | bytes 18436
  173.5 8.2 %copy-start.4 = (f32[384,2,6]{0,2,1:T(8,128)S(1)}, f32[384,2,6]{0,2,1:T(8,128)}, u32[]{:S(2)}) copy-start(f32[384,2,6]{0,2,1:T(8,128)} %get-tuple-element.283) | copy-start | bytes 55300 | tf_op jit(solution)/shard_map/while/body/eval_jaxpr/cond
  206.3 7.9 %copy-start.4 = (f32[384,2,6]{0,2,1:T(8,128)S(1)}, f32[384,2,6]{0,2,1:T(8,128)}, u32[]{:S(2)}) copy-start(f32[384,2,6]{0,2,1:T(8,128)} %get-tuple-element.283) | copy-start | bytes 55300 | tf_op jit(solution)/shard_map/while/body/eval_jaxpr/cond
  238.9 7.9 %copy-start.4 = (f32[384,2,6]{0,2,1:T(8,128)S(1)}, f32[384,2,6]{0,2,1:T(8,128)}, u32[]{:S(2)}) copy-start(f32[384,2,6]{0,2,1:T(8,128)} %get-tuple-element.283) | copy-start | bytes 55300 | tf_op jit(solution)/shard_map/while/body/eval_jaxpr/cond
  271.4 7.9 %copy-start.4 = (f32[384,2,6]{0,2,1:T(8,128)S(1)}, f32[384,2,6]{0,2,1:T(8,128)}, u32[]{:S(2)}) copy-start(f32[384,2,6]{0,2,1:T(8,128)} %get-tuple-element.283) | copy-start | bytes 55300 | tf_op jit(solution)/shard_map/while/body/eval_jaxpr/cond
  304.0 7.9 %copy-start.4 = (f32[384,2,6]{0,2,1:T(8,128)S(1)}, f32[384,2,6]{0,2,1:T(8,128)}, u32[]{:S(2)}) copy-start(f32[384,2,6]{0,2,1:T(8,128)} %get-tuple-element.283) | copy-start | bytes 55300 | tf_op jit(solution)/shard_map/while/body/eval_jaxpr/cond
  336.5 7.9 %copy-start.4 = (f32[384,2,6]{0,2,1:T(8,128)S(1)}, f32[384,2,6]{0,2,1:T(8,128)}, u32[]{:S(2)}) copy-start(f32[384,2,6]{0,2,1:T(8,128)} %get-tuple-element.283) | copy-start | bytes 55300 | tf_op jit(solution)/shard_map/while/body/eval_jaxpr/cond
  374.7 10.2 %copy-start.11 = (pred[16,2,64]{2,1,0:T(4,128)(4,1)S(1)}, pred[16,2,64]{2,1,0:T(4,128)(4,1)}, u32[]{:S(2)}) copy-start(pred[16,2,64]{2,1,0:T(4,128)(4,1)} %broadcast_in_dim.122) | copy-start | bytes 6148
  390.9 35.5 %copy-start.10 = (bf16[2,2,16,768]{3,2,1,0:T(8,128)(2,1)S(1)}, bf16[2,2,16,768]{3,2,1,0:T(8,128)(2,1)}, u32[]{:S(2)}) copy-start(bf16[2,2,16,768]{3,2,1,0:T(8,128)(2,1)} %param.39) | copy-start | bytes 294916
  390.9 35.5 %copy-start.9 = (bf16[2,1536,16]{1,2,0:T(8,128)(2,1)S(1)}, bf16[2,1536,16]{1,2,0:T(8,128)(2,1)}, u32[]{:S(2)}) copy-start(bf16[2,1536,16]{1,2,0:T(8,128)(2,1)} %param.38) | copy-start | bytes 294916
  390.9 140.7 %all-to-all-start = ((bf16[16,2,64,1536]{3,2,1,0:T(8,128)(2,1)}), bf16[16,2,64,1536]{3,2,1,0:T(8,128)(2,1)}, u32[]{:S(2)}, u32[]{:S(2)}) async-start(bf16[16,2,64,1536]{3,2,1,0:T(8,128)(2,1)} %broadcast_select_fusion), calls=%async_computation | async-start | bytes 12582912 | tf_op jit(solution)/shard_map/all_to_all | solution.py:194
  531.6 23.9 %all-to-all-start.1 = ((bf16[16,2,64,256]{3,2,1,0:T(8,128)(2,1)}), bf16[16,2,64,256]{3,2,1,0:T(8,128)(2,1)S(1)}, u32[]{:S(2)}, u32[]{:S(2)}) async-start(bf16[16,2,64,256]{3,2,1,0:T(8,128)(2,1)} %broadcast_select_fusion.1), calls=%async_computation.1 | async-start | bytes 2097152 | tf_op jit(solution)/shard_map/all_to_all | solution.py:195
  573.0 7.9 %copy-start.14 = (s32[1536]{0:T(1024)S(1)}, s32[1536]{0:T(1024)}, u32[]{:S(2)}) copy-start(s32[1536]{0:T(1024)} %copy-done.13) | copy-start | bytes 18436
  573.0 96.8 %all-to-all-start.2 = ((bf16[16,2,64,1536]{3,2,1,0:T(8,128)(2,1)}), bf16[16,2,64,1536]{3,2,1,0:T(8,128)(2,1)}, u32[]{:S(2)}, u32[]{:S(2)}) async-start(bf16[16,2,64,1536]{3,2,1,0:T(8,128)(2,1)} %copy.120), calls=%async_computation.2 | async-start | bytes 12582912 | tf_op jit(solution)/shard_map/all_to_all | solution.py:207
  (21 other events, 126.9 us)
Sparse Core Ops, SparseCore 0:
  9.0 47.1 all-gather.4
  58.0 23.9 all-gather.6
  86.8 59.6 all-gather.8
  148.0 35.6 all-gather.10
where the time goes:
time: 724 us; the launch traced here: 716 us
  waiting for transfers between devices  212 us (29%)
  matrix products  134 us (19%)
  local copies, waits for them, and re-layouts  116 us (16%)
  other arithmetic  106 us (15%)
  blocking collectives  71.7 us (10%)
  starting transfers between devices  50.3 us (7%)
  between operations  14.4 us (2%)
  loops' own time  11.5 us (2%)
    all_to_all x1, waiting for transfers between devices, body(): lax.all_to_all(outputs, 'exp', split_axis=0, concat_axis=0, tiled=True)  88.9 us
    all_to_all x1, waiting for transfers between devices, body(): lax.all_to_all(send_rows, 'exp', split_axis=0, concat_axis=0, tiled=True)  68.9 us
    reduce_sum x6, other arithmetic, online_step(): running_sum = running_sum * factor + jnp.sum(weights, axis=-1)  47.7 us
    dot_general x6, matrix products, online_step(): jnp.einsum('tkgs,skd->tkgd', weights.astype(jnp.bfloat16), value_part, pr...  46.8 us
    dot_general x6, matrix products, online_step(): jnp.einsum('tkgd,skd->tkgs', queries, key_part, preferred_element_type=jn...  38.2 us
    all_to_all x1, starting transfers between devices, body(): lax.all_to_all(send_rows, 'exp', split_axis=0, concat_axis=0, tiled=True)  35.5 us
    all_gather x1, waiting for transfers between devices, body(): lax.all_gather(attention_in, 'req', axis=1, tiled=True)  27.7 us
    all_gather x1, waiting for transfers between devices, body(): lax.all_gather(adapter_in_up, 'req', axis=0, tiled=True)  18.2 us
  transfers between devices with their start and end apart: 7, of which 5 were waited for; matrix products, arithmetic and copies ran while one was open for 38% of the time, Pallas kernels for 0%

commit v1 on v0

--- a/solution.py
+++ b/solution.py
@@ -11,6 +11,28 @@
 CAP = 64
 EPSILON = 1e-06
 NEGATIVE = -1e30
+
+
+def joined_along(blocks, dim):
+    shape = list(blocks.shape[1:])
+    shape[dim] *= blocks.shape[0]
+    return jnp.moveaxis(blocks, 0, dim).reshape(shape)
+
+
+def collect(shard, axis, dim):
+    count = lax.axis_size(axis)
+    pairs = [(i, (i + 1) % count) for i in range(count)]
+    back = [(b, a) for a, b in pairs]
+    lower, upper = ([], [])
+    for step in range(count - 1):
+        if step % 2 == 0:
+            lower.append(lax.ppermute(lower[-1] if lower else shard, axis, pairs))
+        else:
+            upper.append(lax.ppermute(upper[-1] if upper else shard, axis, back))
+    blocks = jnp.stack([*lower[::-1], shard, *upper])
+    shift = lax.axis_index(axis) - len(lower)
+    blocks = blocks[(jnp.arange(count) - shift) % count]
+    return joined_along(blocks, dim)
 
 
 def scaled_norm(inputs, gain):
@@ -107,7 +129,7 @@
     held_factors = (
         lax.all_gather(adapter_in_down, "req", axis=0, tiled=True),
         lax.all_gather(adapter_in_up, "req", axis=0, tiled=True),
-        lax.all_gather(adapter_out_down, "req", axis=0, tiled=True),
+        collect(adapter_out_down, "req", 0),
         lax.all_gather(adapter_out_up, "req", axis=0, tiled=True),
         lax.all_gather(adapter_expert_down, "req", axis=0, tiled=True),
         lax.all_gather(adapter_expert_up, "req", axis=0, tiled=True),

time: 724 us -> 692 us (0.956)
  local copies, waits for them, and re-layouts: 116 us -> 100 us
  other arithmetic: 106 us -> 91.3 us
  blocking collectives: 71.7 us -> 58.1 us
  starting transfers between devices: 50.3 us -> 57.7 us
    all_gather x1 -> x0, blocking collectives: 14.4 us -> none  [body(): lax.all_gather(adapter_out_down, 'req', axis=0, tiled=True)]
    ppermute x0 -> x7, starting transfers between devices: none -> 9.67 us  [the longest x3 9.06 us: collect(): upper.append(lax.ppermute(upper[-1] if upper else shard, axis, back))]
    ppermute x0 -> x7, waiting for transfers between devices: none -> 7.94 us  [the longest x4 7.69 us: collect(): lower.append(lax.ppermute(lower[-1] if lower else shard, axis, pairs))]
    another operation x8 -> x9, local copies, waits for them, and re-layouts: 8.72 us -> 1.33 us
  transfers between devices with their start and end apart: 7 -> 14, of which waited for: 5 -> 9; matrix products, arithmetic and copies ran while one was open for 38% -> 34% of each run, Pallas kernels for 0% -> 0%
where the time goes in v1:
time: 692 us; the launch traced here: 685 us
  waiting for transfers between devices  217 us (31%)
  matrix products  136 us (20%)
  local copies, waits for them, and re-layouts  100 us (14%)
  other arithmetic  91.3 us (13%)
  blocking collectives  58.1 us (8%)
  starting transfers between devices  57.7 us (8%)
  between operations  14.4 us (2%)
  loops' own time  10.5 us (2%)
    all_to_all x1, waiting for transfers between devices, body(): lax.all_to_all(outputs, 'exp', split_axis=0, concat_axis=0, tiled=True)  88.4 us
    all_to_all x1, waiting for transfers between devices, body(): lax.all_to_all(send_rows, 'exp', split_axis=0, concat_axis=0, tiled=True)  68.3 us
    reduce_sum x6, other arithmetic, online_step(): running_sum = running_sum * factor + jnp.sum(weights, axis=-1)  48.7 us
    dot_general x6, matrix products, online_step(): jnp.einsum('tkgs,skd->tkgd', weights.astype(jnp.bfloat16), value_part, pr...  47.3 us
    dot_general x6, matrix products, online_step(): jnp.einsum('tkgd,skd->tkgs', queries, key_part, preferred_element_type=jn...  38.2 us
    all_to_all x1, starting transfers between devices, body(): lax.all_to_all(send_rows, 'exp', split_axis=0, concat_axis=0, tiled=True)  33.2 us
    all_gather x1, waiting for transfers between devices, body(): lax.all_gather(attention_in, 'req', axis=1, tiled=True)  27.9 us
    all_gather x1, waiting for transfers between devices, body(): lax.all_gather(adapter_in_up, 'req', axis=0, tiled=True)  18.4 us
  transfers between devices with their start and end apart: 14, of which 9 were waited for; matrix products, arithmetic and copies ran while one was open for 34% of the time, Pallas kernels for 0%

profile of v1, /device:TPU:100, one launch (start us, length us, event | category | flops | bytes accessed | tf_op | source)
XLA Modules:
  0.0 685.4 jit_solution(15473120292377303434)
XLA Ops:
  11.5 16.0 %all_gather.25 = bf16[16,1536,16]{1,2,0:T(8,128)(2,1)} all-gather(bf16[2,1536,16]{1,2,0:T(8,128)(2,1)} %param.34), channel_id=1, replica_groups=mesh['req'=8,'exp'=16] {'req'}, dimensions={0}, use_global_device_ids=true | all-gather | bytes 884736 | tf_op jit(solution)/shard_map/all_gather | solution.py:130
  27.5 27.9 %all-gather.5.cloned.1.call-done = bf16[1536,2048]{1,0:T(8,128)(2,1)} async-done(((bf16[1536,256]{1,0:T(8,128)(2,1)}), bf16[1536,2048]{1,0:T(8,128)(2,1)}) %all-gather.5.cloned.1.call-update) | async-done | bytes 6291472 | tf_op jit(solution)/shard_map/all_gather | solution.py:141
  62.9 18.4 %all-gather.7.cloned.1.call-done = bf16[16,16,2048]{2,1,0:T(8,128)(2,1)} async-done(((bf16[2,16,2048]{2,1,0:T(8,128)(2,1)}), bf16[16,16,2048]{2,1,0:T(8,128)(2,1)}) %all-gather.7.cloned.1.call-update) | async-done | bytes 1048592 | tf_op jit(solution)/shard_map/all_gather | solution.py:131
  90.3 9.1 %reduce-window.27 = s32[32,12,128]{2,1,0:T(8,128)S(1)} reduce-window(s32[32,12,128]{2,1,0:T(8,128)S(1)} %fusion.45, s32[]{:T(128)} %copy.163), window={size=1x1x128 pad=0_0x0_0x127_0}, to_apply=%region_12.13 | reduce-window | flops 6242304 | bytes 393220 | tf_op jit(solution)/shard_map/reduce-window.2
  106.7 14.9 %all_gather.29 = bf16[16,16,1536]{2,1,0:T(8,128)(2,1)} all-gather(bf16[2,16,1536]{2,1,0:T(8,128)(2,1)S(1)} %copy-done.4), channel_id=1, replica_groups=mesh['req'=8,'exp'=16] {'req'}, dimensions={0}, use_global_device_ids=true | all-gather | bytes 884736 | tf_op jit(solution)/shard_map/all_gather | solution.py:133
  146.1 8.6 %copy.108 = bf16[8,768,512]{1,2,0:T(8,128)(2,1)} copy(bf16[8,768,512]{2,1,0:T(8,128)(2,1)} %bitcast.132) | data formatting | bytes 12582912 | tf_op jit(solution)/shard_map/while | solution.py:181
  156.5 177.3 %while.18 = (s32[]{:T(128)}, f32[384,2,6]{0,2,1:T(8,128)S(1)}, f32[384,2,6]{0,2,1:T(8,128)S(1)}, f32[384,2,6,128]{3,0,2,1:T(8,128)}, s32[8]{0:T(128)S(1)}, /*ind...) while((s32[]{:T(128)}, f32[384,2,6]{0,2,1:T(8,128)S(1)}, ...), condition=%wide.region_11.12_spmd, body=%wide.region_4.11_spmd.sunk | while | flops 1854454528 | bytes 72678240 | solution.py:181
  158.9 26.8 %conditional.2 = ((f32[384,2,6]{0,2,1:T(8,128)S(1)}, f32[384,2,6]{0,2,1:T(8,128)S(1)}, f32[384,2,6,128]{3,0,2,1:T(8,128)})) conditional(s32[]{:T(128)} %convert_element_type.156, (f32[384,2,6]{0,2,1:T(8,128)S(1)}, f32[384,2,6]{0,2,1:T(8,128)S(1)}, f32[384,2,6,128]{3,0,2,1:T(8,128)}) %tuple.62, (s32[]{:T(128)}, s32[768]{0:T(1024)S(1)}, ...), branch_computations={%region_5.5_spmd, %region_6.10_spmd} | conditional | flops 1854454528 | bytes 72674856 | solution.py:179
  188.1 26.2 %conditional.2 = ((f32[384,2,6]{0,2,1:T(8,128)S(1)}, f32[384,2,6]{0,2,1:T(8,128)S(1)}, f32[384,2,6,128]{3,0,2,1:T(8,128)})) conditional(s32[]{:T(128)} %convert_element_type.156, (f32[384,2,6]{0,2,1:T(8,128)S(1)}, f32[384,2,6]{0,2,1:T(8,128)S(1)}, f32[384,2,6,128]{3,0,2,1:T(8,128)}) %tuple.62, (s32[]{:T(128)}, s32[768]{0:T(1024)S(1)}, ...), branch_computations={%region_5.5_spmd, %region_6.10_spmd} | conditional | flops 1854454528 | bytes 72674856 | solution.py:179
  216.8 26.2 %conditional.2 = ((f32[384,2,6]{0,2,1:T(8,128)S(1)}, f32[384,2,6]{0,2,1:T(8,128)S(1)}, f32[384,2,6,128]{3,0,2,1:T(8,128)})) conditional(s32[]{:T(128)} %convert_element_type.156, (f32[384,2,6]{0,2,1:T(8,128)S(1)}, f32[384,2,6]{0,2,1:T(8,128)S(1)}, f32[384,2,6,128]{3,0,2,1:T(8,128)}) %tuple.62, (s32[]{:T(128)}, s32[768]{0:T(1024)S(1)}, ...), branch_computations={%region_5.5_spmd, %region_6.10_spmd} | conditional | flops 1854454528 | bytes 72674856 | solution.py:179
  245.4 26.2 %conditional.2 = ((f32[384,2,6]{0,2,1:T(8,128)S(1)}, f32[384,2,6]{0,2,1:T(8,128)S(1)}, f32[384,2,6,128]{3,0,2,1:T(8,128)})) conditional(s32[]{:T(128)} %convert_element_type.156, (f32[384,2,6]{0,2,1:T(8,128)S(1)}, f32[384,2,6]{0,2,1:T(8,128)S(1)}, f32[384,2,6,128]{3,0,2,1:T(8,128)}) %tuple.62, (s32[]{:T(128)}, s32[768]{0:T(1024)S(1)}, ...), branch_computations={%region_5.5_spmd, %region_6.10_spmd} | conditional | flops 1854454528 | bytes 72674856 | solution.py:179
  274.1 26.2 %conditional.2 = ((f32[384,2,6]{0,2,1:T(8,128)S(1)}, f32[384,2,6]{0,2,1:T(8,128)S(1)}, f32[384,2,6,128]{3,0,2,1:T(8,128)})) conditional(s32[]{:T(128)} %convert_element_type.156, (f32[384,2,6]{0,2,1:T(8,128)S(1)}, f32[384,2,6]{0,2,1:T(8,128)S(1)}, f32[384,2,6,128]{3,0,2,1:T(8,128)}) %tuple.62, (s32[]{:T(128)}, s32[768]{0:T(1024)S(1)}, ...), branch_computations={%region_5.5_spmd, %region_6.10_spmd} | conditional | flops 1854454528 | bytes 72674856 | solution.py:179
  302.7 26.2 %conditional.2 = ((f32[384,2,6]{0,2,1:T(8,128)S(1)}, f32[384,2,6]{0,2,1:T(8,128)S(1)}, f32[384,2,6,128]{3,0,2,1:T(8,128)})) conditional(s32[]{:T(128)} %convert_element_type.156, (f32[384,2,6]{0,2,1:T(8,128)S(1)}, f32[384,2,6]{0,2,1:T(8,128)S(1)}, f32[384,2,6,128]{3,0,2,1:T(8,128)}) %tuple.62, (s32[]{:T(128)}, s32[768]{0:T(1024)S(1)}, ...), branch_computations={%region_5.5_spmd, %region_6.10_spmd} | conditional | flops 1854454528 | bytes 72674856 | solution.py:179
  347.8 10.3 %gather_fusion.1 = bf16[2048,1536]{1,0:T(8,128)(2,1)} fusion(bf16[384,1536]{1,0:T(8,128)(2,1)S(1)} %fusion.32, s32[2048]{0:T(1024)S(1)} %fusion.54), kind=kCustom, calls=%fused_computation.1 | custom fusion | bytes 12591104 | tf_op jit(solution)/shard_map/gather | solution.py:207
  364.0 33.2 %all-to-all-start = ((bf16[16,2,64,1536]{3,2,1,0:T(8,128)(2,1)}), bf16[16,2,64,1536]{3,2,1,0:T(8,128)(2,1)}, u32[]{:S(2)}, u32[]{:S(2)}) async-start(bf16[16,2,64,1536]{3,2,1,0:T(8,128)(2,1)} %broadcast_select_fusion), calls=%async_computation | async-start | bytes 12582912 | tf_op jit(solution)/shard_map/all_to_all | solution.py:216
  397.3 13.8 %all_gather.30 = bf16[16,1536,16]{1,2,0:T(8,128)(2,1)S(1)} all-gather(bf16[2,1536,16]{1,2,0:T(8,128)(2,1)S(1)} %copy-done.5), channel_id=1, replica_groups=mesh['req'=8,'exp'=16] {'req'}, dimensions={0}, use_global_device_ids=true | all-gather | bytes 884736 | tf_op jit(solution)/shard_map/all_gather | solution.py:134
  411.0 13.4 %all_gather.31 = bf16[16,2,16,768]{3,2,0,1:T(8,128)(2,1)S(1)} all-gather(bf16[2,2,16,768]{3,2,0,1:T(8,128)(2,1)S(1)} %copy.118), channel_id=1, replica_groups=mesh['req'=8,'exp'=16] {'req'}, dimensions={0}, use_global_device_ids=true | all-gather | bytes 884736 | tf_op jit(solution)/shard_map/all_gather | solution.py:135
  433.7 68.3 %all-to-all-done = bf16[16,2,64,1536]{3,2,1,0:T(8,128)(2,1)} async-done(((bf16[16,2,64,1536]{3,2,1,0:T(8,128)(2,1)}), bf16[16,2,64,1536]{3,2,1,0:T(8,128)(2,1)}, u32[]{:S(2)}, u32[]{:S(2)}) %all-to-all-start) | async-done | bytes 6291488 | tf_op jit(solution)/shard_map/all_to_all | solution.py:216
  508.9 17.0 %fusion.15 = f32[16,2,64,1536]{3,2,0,1:T(8,128)} fusion(bf16[2,1536,1536]{2,1,0:T(8,128)(2,1)} %param.32, bf16[16,2,64,1536]{3,2,1,0:T(8,128)(2,1)} %all-to-all-done), kind=kOutput, calls=%fused_computation.29 | convolution fusion | flops 9663676416 | bytes 28311552 | tf_op jit(solution)/shard_map/necd,edf->necf/dot_general | solution.py:219
  525.9 11.3 %convert_bitcast_fusion = bf16[16,2,64,1536]{3,2,0,1:T(8,128)(2,1)} fusion(bf16[2,768,1536]{2,1,0:T(8,128)(2,1)} %param.33, f32[16,2,64,1536]{3,2,0,1:T(8,128)} %fusion.15, bf16[2,256,768,1]{2,1,3,0:T(8,128)(2,1)S(1)} %bitcast.141, bf16[16,2,64,256]{3,2,1,0:T(8,128)(2,1)S(1)} %all-to-all-done.1), kind=kOutput, calls=%fused_computation.35 | convolution fusion | flops 5646581760 | bytes 25427968 | tf_op jit(solution)/shard_map/necf,efd->necd/dot_general | solution.py:226
  551.3 88.4 %all-to-all-done.2 = bf16[16,2,64,1536]{3,2,1,0:T(8,128)(2,1)} async-done(((bf16[16,2,64,1536]{3,2,1,0:T(8,128)(2,1)}), bf16[16,2,64,1536]{3,2,1,0:T(8,128)(2,1)}, u32[]{:S(2)}, u32[]{:S(2)}) %all-to-all-start.2) | async-done | bytes 6291488 | tf_op jit(solution)/shard_map/all_to_all | solution.py:229
  639.7 14.0 %gather_fusion.3 = bf16[1536,1536]{1,0:T(8,128)(2,1)} fusion(bf16[2048,1536]{1,0:T(8,128)(2,1)} %bitcast.50, s32[2048]{0:T(1024)S(1)} %pad_clamp_fusion), kind=kCustom, calls=%fused_computation.3 | custom fusion | bytes 9443328 | tf_op jit(solution)/shard_map/gather | solution.py:231
  653.7 9.7 %reshape.352 = f32[384,4,1536]{2,1,0:T(4,128)} reshape(bf16[1536,1536]{1,0:T(8,128)(2,1)} %gather_fusion.3) | data formatting | bytes 14155776 | tf_op jit(solution)/shard_map/convert_element_type | solution.py:231
  663.4 12.3 %multiply_reduce_fusion = f32[384,1536]{1,0:T(8,128)} fusion(f32[384,4,1536]{2,1,0:T(4,128)} %reshape.352, f32[384,4]{1,0:T(8,128)S(1)} %copy.111), kind=kLoop, calls=%fused_computation.28 | loop fusion | flops 4128768 | bytes 11802624 | tf_op jit(solution)/shard_map/reduce_sum | solution.py:232
  (262 shorter events, 273.8 us)
Async XLA Ops:
  6.5 48.9 %all-gather.5.cloned.1.call-start = ((), (), s32[]{:S(2)}) async-start(), calls=%async_computation.3 | async-start | bytes 7077888 | tf_op jit(solution)/shard_map/all_gather | solution.py:141
  7.3 74.1 %all-gather.7.cloned.1.call-start = ((), (), s32[]{:S(2)}) async-start(), calls=%async_computation.4 | async-start | bytes 1179648 | tf_op jit(solution)/shard_map/all_gather | solution.py:131
  8.0 138.1 %all-gather.9.cloned.1.call-start = ((), (), s32[]{:S(2)}) async-start(), calls=%async_computation.5 | async-start | bytes 6684672 | tf_op jit(solution)/shard_map/all_gather | solution.py:157
  27.5 53.9 %copy-start.2 = (bf16[384,1536]{1,0:T(8,128)(2,1)S(1)}, bf16[384,1536]{1,0:T(8,128)(2,1)}, u32[]{:S(2)}) copy-start(bf16[384,1536]{1,0:T(8,128)(2,1)} %param.22) | copy-start | bytes 3538948
  27.5 53.9 %copy-start.13 = (f32[1536]{0:T(1024)S(1)}, f32[1536]{0:T(1024)}, u32[]{:S(2)}) copy-start(f32[1536]{0:T(1024)} %param.27) | copy-start | bytes 18436
  81.4 8.5 %copy-start.10 = (s32[384,4]{0,1:T(4,128)S(1)}, s32[384,4]{0,1:T(4,128)}, u32[]{:S(2)}) copy-start(s32[384,4]{0,1:T(4,128)} %param.25) | copy-start | bytes 18436
  85.5 21.2 %copy-start.4 = (bf16[2,16,1536]{2,1,0:T(8,128)(2,1)S(1)}, bf16[2,16,1536]{2,1,0:T(8,128)(2,1)}, u32[]{:S(2)}) copy-start(bf16[2,16,1536]{2,1,0:T(8,128)(2,1)} %param.37) | copy-start | bytes 294916
  85.5 37.0 %copy-start.15 = (f32[12]{0:T(128)S(1)}, f32[12]{0:T(128)}, u32[]{:S(2)}) copy-start(f32[12]{0:T(128)} %param.29) | copy-start | bytes 148
  86.3 251.0 %all-gather.11.cloned.1.call-start = ((), (), s32[]{:S(2)}) async-start(), calls=%async_computation.6 | async-start | bytes 5308416 | tf_op jit(solution)/shard_map/all_gather | solution.py:142
  86.9 34.7 %collective-permute-start = (bf16[2,1536,16]{1,2,0:T(8,128)(2,1)S(1)}, bf16[2,1536,16]{1,2,0:T(8,128)(2,1)S(1)}, u32[]{:S(2)}, u32[]{:S(2)}) collective-permute-start(bf16[2,1536,16]{1,2,0:T(8,128)(2,1)S(1)} %copy-done.6), channel_id=1, source_target_pairs={{0,16},{16,32},{32,48},{48,64},{64,80},{80,96},{96,112},{112,0},{1... | collective-permute-start | bytes 294920 | tf_op jit(solution)/shard_map/ppermute | solution.py:29
  87.2 39.8 %collective-permute-start.4 = (bf16[2,1536,16]{1,2,0:T(8,128)(2,1)S(1)}, bf16[2,1536,16]{1,2,0:T(8,128)(2,1)S(1)}, u32[]{:S(2)}, u32[]{:S(2)}) collective-permute-start(bf16[2,1536,16]{1,2,0:T(8,128)(2,1)S(1)} %copy-done.6), channel_id=1, source_target_pairs={{16,0},{32,16},{48,32},{64,48},{80,64},{96,80},{112,96},{0,112},{1... | collective-permute-start | bytes 294920 | tf_op jit(solution)/shard_map/ppermute | solution.py:31
  100.4 37.9 %copy-start.8 = (s32[1536]{0:T(1024)}, s32[1536]{0:T(1024)S(1)}, u32[]{:S(2)}) copy-start(s32[1536]{0:T(1024)S(1)} %fusion.56) | copy-start | bytes 18436
  121.6 5.3 collective-permute-start.1
  126.9 5.3 collective-permute-start.2
  126.9 5.2 collective-permute-start.5
  132.1 5.3 collective-permute-start.3
  132.2 5.6 collective-permute-start.6
  146.1 10.4 %copy-start.11 = (s32[1,16]{1,0:T(1,128)S(1)}, s32[1,16]{1,0:T(1,128)}, u32[]{:S(2)}) copy-start(s32[1,16]{1,0:T(1,128)} %param.23) | copy-start | bytes 196
  167.9 8.4 %copy-start = (f32[384,2,6,128]{3,0,2,1:T(8,128)S(1)}, f32[384,2,6,128]{3,0,2,1:T(8,128)}, u32[]{:S(2)}) copy-start(f32[384,2,6,128]{3,0,2,1:T(8,128)} %get-tuple-element.284) | copy-start | bytes 7077892 | tf_op jit(solution)/shard_map/while/body/eval_jaxpr/cond
  364.0 33.3 %copy-start.7 = (bf16[2,2,16,768]{3,2,1,0:T(8,128)(2,1)S(1)}, bf16[2,2,16,768]{3,2,1,0:T(8,128)(2,1)}, u32[]{:S(2)}) copy-start(bf16[2,2,16,768]{3,2,1,0:T(8,128)(2,1)} %param.39) | copy-start | bytes 294916
  364.0 33.3 %copy-start.5 = (bf16[2,1536,16]{1,2,0:T(8,128)(2,1)S(1)}, bf16[2,1536,16]{1,2,0:T(8,128)(2,1)}, u32[]{:S(2)}) copy-start(bf16[2,1536,16]{1,2,0:T(8,128)(2,1)} %param.38) | copy-start | bytes 294916
  364.0 138.0 %all-to-all-start = ((bf16[16,2,64,1536]{3,2,1,0:T(8,128)(2,1)}), bf16[16,2,64,1536]{3,2,1,0:T(8,128)(2,1)}, u32[]{:S(2)}, u32[]{:S(2)}) async-start(bf16[16,2,64,1536]{3,2,1,0:T(8,128)(2,1)} %broadcast_select_fusion), calls=%async_computation | async-start | bytes 12582912 | tf_op jit(solution)/shard_map/all_to_all | solution.py:216
  502.0 23.9 %all-to-all-start.1 = ((bf16[16,2,64,256]{3,2,1,0:T(8,128)(2,1)}), bf16[16,2,64,256]{3,2,1,0:T(8,128)(2,1)S(1)}, u32[]{:S(2)}, u32[]{:S(2)}) async-start(bf16[16,2,64,256]{3,2,1,0:T(8,128)(2,1)} %broadcast_select_fusion.1), calls=%async_computation.1 | async-start | bytes 2097152 | tf_op jit(solution)/shard_map/all_to_all | solution.py:217
  543.4 96.3 %all-to-all-start.2 = ((bf16[16,2,64,1536]{3,2,1,0:T(8,128)(2,1)}), bf16[16,2,64,1536]{3,2,1,0:T(8,128)(2,1)}, u32[]{:S(2)}, u32[]{:S(2)}) async-start(bf16[16,2,64,1536]{3,2,1,0:T(8,128)(2,1)} %copy.120), calls=%async_computation.2 | async-start | bytes 12582912 | tf_op jit(solution)/shard_map/all_to_all | solution.py:229
  (16 other events, 80.5 us)
Sparse Core Ops, SparseCore 0:
  9.0 46.3 all-gather.4
  57.1 24.2 all-gather.6
  86.4 59.5 all-gather.8
  147.6 35.6 all-gather.10
